TPU v7x, 32 devices: a whole 2x2x4 slice. The times are simulated.
32 devices in a mesh: grp: 2 (over x), scan: 8 (over z, y), det: 2 (over core).
Axes of the slice: x: 2, y: 2, z: 4, core: 2. Of those that a mesh axis runs over, the one named last changes fastest.
Arguments:
- spectra: float32 [16384, 4096], P(('grp', 'scan'), 'det'), parts along dimension 0, may hold values from 0 to 544, as said below
- basis: float32 [64, 4096], P('grp', 'det'), parts along dimension 0, may hold values from 0.03 to 8, as said below
- loadings: float32 [64, 8192], P('grp', 'scan'), parts along dimension 0, may hold values from 0.005 to 6, as said below
Outputs:
- new_loadings: float32 [64, 8192], P('grp', 'scan'), parts along dimension 0
- new_basis: float32 [64, 4096], P('grp', 'det'), parts along dimension 0
There are 2 independent parts, one for each index of `grp`. A program takes and returns all parts, laid end to end along the dimension named above; each array names one. Nothing has to cross between parts.
Inputs may be any that keep to these rules, and one draw needn't show every extreme that they name: `spectra`: intensities are nonnegative. `basis`: entries are positive. `loadings`: entries are positive.
All inputs are finite; a program needn't handle non-finite values.
Results may differ from a plain program's by a relative error of at most 0.00005.
Values sent between devices are 32-bit elements; how exact they have to be, the bound alone decides.
A program may use at most 64 MiB of HBM per device.

v0:
```python
import jax
import jax.numpy as jnp
from jax import lax
from jax.sharding import PartitionSpec as P

HIGHEST = lax.Precision.HIGHEST


def swapped(block, axis, stride):
    count = lax.axis_size(axis)
    route = []
    for low in range(count):
        high = low | 1 << stride
        if high != low and high < count:
            route += [(low, high), (high, low)]
    return lax.ppermute(block, axis, route)


def per_device(spectra, basis, loadings):
    partner = swapped(basis, "det", 0)
    tied = 0.5 * (basis + jnp.flip(partner, 1))
    local_numer = lax.dot_general(tied, spectra, (((1,), (1,)), ((), ())), precision=HIGHEST)
    gram = 2.0 * lax.dot_general(tied, tied, (((1,), (1,)), ((), ())), precision=HIGHEST)
    numer_h = lax.psum(local_numer, "det")
    new_loadings = loadings * numer_h / jnp.dot(gram, loadings, precision=HIGHEST)
    w_terms = jnp.dot(new_loadings, spectra, precision=HIGHEST)
    cross_terms = lax.dot_general(
        new_loadings, new_loadings, (((1,), (1,)), ((), ())), precision=HIGHEST
    )
    numer_w, cross = lax.psum((w_terms, cross_terms), "scan")
    mirrored = swapped(numer_w, "det", 0)
    tied_numer = 0.5 * (numer_w + jnp.flip(mirrored, 1))
    new_basis = tied * tied_numer / jnp.dot(cross, tied, precision=HIGHEST)
    return (new_loadings, new_basis)


def solution(mesh):
    in_specs = (P(("grp", "scan"), "det"), P("grp", "det"), P("grp", "scan"))
    out_specs = (P("grp", "scan"), P("grp", "det"))
    return jax.shard_map(
        per_device, mesh=mesh, in_specs=in_specs, out_specs=out_specs, check_vma=False
    )
```

profile of v0, /device:TPU:0, one launch (start us, length us, event | category | flops | bytes accessed | tf_op | source)
XLA Modules:
  0.0 169.7 jit_solution(7217789478776410331)
XLA Ops:
  7.2 0.0 copy-start.1
  7.2 0.0 all-reduce.3.cloned.1.call-start
  7.2 0.6 collective-permute-start
  7.8 1.4 collective-permute-done
  9.2 1.2 rev.7
  10.3 1.0 add_multiply_fusion
  11.3 10.6 %fusion = f32[32,1024]{1,0:T(8,128)} fusion(f32[32,2048]{1,0:T(8,128)S(1)} %add_multiply_fusion, f32[1024,2048]{1,0:T(8,128)} %param.3), kind=kOutput, calls=%fused_computation.4 | convolution fusion | flops 805306368 | bytes 8781824 | tf_op jit(solution)/shard_map/dot_general | solution.py:22
  21.9 0.0 all-reduce.3.cloned.1.call-update
  21.9 0.0 all-reduce.5.cloned.1.call-start
  22.0 0.3 convolution_multiply_fusion
  22.3 20.3 %all-reduce.3.cloned.1.call-done = f32[32,1024]{1,0:T(8,128)} async-done(((f32[32,1024]{1,0:T(8,128)}), f32[32,1024]{1,0:T(8,128)}) %all-reduce.3.cloned.1.call-update) | async-done | bytes 131088 | tf_op jit(solution)/shard_map/psum | solution.py:24
  42.6 0.0 copy-done.1
  42.6 1.2 convolution_divide_fusion
  43.8 0.0 copy-start
  43.8 7.9 %fusion.1 = f32[32,2048]{1,0:T(8,128)} fusion(f32[32,1024]{1,0:T(8,128)S(1)} %convolution_divide_fusion, f32[1024,2048]{1,0:T(8,128)} %param.3), kind=kOutput, calls=%fused_computation.5 | convolution fusion | flops 805306368 | bytes 8781824 | tf_op jit(solution)/shard_map/dot_general | solution.py:26
  51.7 0.0 all-reduce.5.cloned.1.call-update
  51.7 72.4 %all-reduce.5.cloned.1.call-done = f32[32,2048]{1,0:T(8,128)} async-done(((f32[32,2048]{1,0:T(8,128)}), f32[32,2048]{1,0:T(8,128)}) %all-reduce.5.cloned.1.call-update) | async-done | bytes 262160 | tf_op jit(solution)/shard_map/psum | solution.py:30
  124.1 0.0 collective-permute-start.1
  124.1 0.2 fusion.2
  124.3 35.3 %psum.23 = f32[32,32]{1,0:T(8,128)S(1)} all-reduce(f32[32,32]{1,0:T(8,128)S(1)} %fusion.2), channel_id=1, replica_groups=mesh['grp'=2,'scan'=8,'det'=2] {'scan'}, use_global_device_ids=true, to_apply=%region_2.3 | all-reduce | flops 1024 | bytes 8192 | tf_op jit(solution)/shard_map/psum | solution.py:30
  159.7 0.0 collective-permute-done.1
  159.7 1.2 rev.8
  160.8 2.0 %multiply_divide_fusion = f32[32,2048]{1,0:T(8,128)} fusion(f32[32,2048]{1,0:T(8,128)S(1)} %add_multiply_fusion, f32[32,2048]{1,0:T(8,128)} %all-reduce.5.cloned.1.call-done, f32[32,2048]{1,0:T(8,128)S(1)} %rev.8, f32[32,32]{1,0:T(8,128)S(1)} %psum.23), kind=kOutput, calls=%fused_computation.2 | convolution fusion | flops 25427968 | bytes 1052672 | tf_op jit(solution)/shard_map/dot_general | solution.py:33
  162.9 0.0 copy-done
Async XLA Ops:
  7.2 35.4 %copy-start.1 = (f32[32,1024]{1,0:T(8,128)S(1)}, f32[32,1024]{1,0:T(8,128)}, u32[]{:S(2)}) copy-start(f32[32,1024]{1,0:T(8,128)} %param.5) | copy-start | bytes 393220
  7.2 35.4 %all-reduce.3.cloned.1.call-start = ((), (), s32[]{:S(2)}) async-start(), calls=%async_computation | async-start | bytes 262144 | tf_op jit(solution)/shard_map/psum | solution.py:24
  7.2 1.9 %collective-permute-start = (f32[32,2048]{1,0:T(8,128)}, f32[32,2048]{1,0:T(8,128)S(1)}, u32[]{:S(2)}, u32[]{:S(2)}) collective-permute-start(f32[32,2048]{1,0:T(8,128)} %param.4), channel_id=1, source_target_pairs={{0,1},{1,0},{2,3},{3,2},{4,5},{5,4},{6,7},{7,6},{8,9},{9,8},{10,11... | collective-permute-start | bytes 786440 | tf_op jit(solution)/shard_map/ppermute | solution.py:16
  21.9 102.2 %all-reduce.5.cloned.1.call-start = ((), (), s32[]{:S(2)}) async-start(), calls=%async_computation.1 | async-start | bytes 524288 | tf_op jit(solution)/shard_map/psum | solution.py:30
  43.8 119.1 %copy-start = (f32[32,1024]{1,0:T(8,128)}, f32[32,1024]{1,0:T(8,128)S(1)}, u32[]{:S(2)}) copy-start(f32[32,1024]{1,0:T(8,128)S(1)} %convolution_divide_fusion) | copy-start | bytes 393220
  124.1 35.6 %collective-permute-start.1 = (f32[32,2048]{1,0:T(8,128)}, f32[32,2048]{1,0:T(8,128)S(1)}, u32[]{:S(2)}, u32[]{:S(2)}) collective-permute-start(f32[32,2048]{1,0:T(8,128)} %all-reduce.5.cloned.1.call-done), channel_id=1, source_target_pairs={{0,1},{1,0},{2,3},{3,2},{4,5},{5,4},{6,7},{7,6},{8,9},{9,8},{10,11... | collective-permute-start | bytes 786440 | tf_op jit(solution)/shard_map/ppermute | solution.py:16
Sparse Core Ops, SparseCore 0:
  22.0 20.5 all-reduce.2
  51.8 72.1 all-reduce.4
where the time goes:
time: 170 us
  waiting for transfers between devices  94 us (55%)
  blocking collectives  35.3 us (21%)
  matrix products  22.3 us (13%)
  between operations  14.1 us (8%)
  local copies, waits for them, and re-layouts  2.34 us (1%)
    psum x1, waiting for transfers between devices, per_device(): numer_w, cross = lax.psum((w_terms, cross_terms), 'scan')  72.4 us
    psum x1, blocking collectives, per_device(): numer_w, cross = lax.psum((w_terms, cross_terms), 'scan')  35.3 us
    psum x1, waiting for transfers between devices, per_device(): numer_h = lax.psum(local_numer, 'det')  20.3 us
    dot_general x1, matrix products, per_device(): lax.dot_general(tied, spectra, (((1,), (1,)), ((), ())), precision=HIGHEST)  10.6 us
    dot_general x1, matrix products, per_device(): w_terms = jnp.dot(new_loadings, spectra, precision=HIGHEST)  7.91 us
  transfers between devices with their start and end apart: 4, of which 3 were waited for; matrix products, arithmetic and copies ran while one was open for 0% of the time, Pallas kernels for 0%

commit v1 on v0

--- a/solution.py
+++ b/solution.py
@@ -17,11 +17,16 @@
 
 
 def per_device(spectra, basis, loadings):
+
+    def _connect_members_all(z_in):
+        n_now = lax.all_gather(z_in, axis_name="det")
+        return jnp.sum(n_now, axis=0)
+
     partner = swapped(basis, "det", 0)
     tied = 0.5 * (basis + jnp.flip(partner, 1))
     local_numer = lax.dot_general(tied, spectra, (((1,), (1,)), ((), ())), precision=HIGHEST)
     gram = 2.0 * lax.dot_general(tied, tied, (((1,), (1,)), ((), ())), precision=HIGHEST)
-    numer_h = lax.psum(local_numer, "det")
+    numer_h = _connect_members_all(local_numer)
     new_loadings = loadings * numer_h / jnp.dot(gram, loadings, precision=HIGHEST)
     w_terms = jnp.dot(new_loadings, spectra, precision=HIGHEST)
     cross_terms = lax.dot_general(

time: 170 us -> 152 us (0.89)
  waiting for transfers between devices: 94 us -> 75.1 us
  blocking collectives: 35.3 us -> 37.3 us
    psum x1 -> x0, waiting for transfers between devices: 20.3 us -> none  [per_device(): numer_h = lax.psum(local_numer, 'det')]
    all_gather x0 -> x1, blocking collectives: none -> 2 us  [_connect_members_all(): n_now = lax.all_gather(z_in, axis_name='det')]
  transfers between devices with their start and end apart: 4 -> 3, of which waited for: 3 -> 2; matrix products, arithmetic and copies ran while one was open for 0% -> 0% of each run, Pallas kernels for 0% -> 0%
where the time goes in v1:
time: 152 us; the launch traced here: 151 us
  waiting for transfers between devices  75.1 us (49%)
  blocking collectives  37.3 us (25%)
  matrix products  20.8 us (14%)
  between operations  14.1 us (9%)
  local copies, waits for them, and re-layouts  2.34 us (2%)
    psum x1, waiting for transfers between devices, per_device(): numer_w, cross = lax.psum((w_terms, cross_terms), 'scan')  73.7 us
    psum x1, blocking collectives, per_device(): numer_w, cross = lax.psum((w_terms, cross_terms), 'scan')  35.3 us
    dot_general x1, matrix products, per_device(): lax.dot_general(tied, spectra, (((1,), (1,)), ((), ())), precision=HIGHEST)  9.97 us
    dot_general x1, matrix products, per_device(): w_terms = jnp.dot(new_loadings, spectra, precision=HIGHEST)  7.91 us
  transfers between devices with their start and end apart: 3, of which 2 were waited for; matrix products, arithmetic and copies ran while one was open for 0% of the time, Pallas kernels for 0%

profile of v1, /device:TPU:0, one launch (start us, length us, event | category | flops | bytes accessed | tf_op | source)
XLA Modules:
  0.0 151.3 jit_solution(17699069668944774600)
XLA Ops:
  7.2 0.0 copy-start.1
  7.2 0.0 all-reduce.2.cloned.1.call-start
  7.2 0.6 collective-permute-start
  7.8 1.4 collective-permute-done
  9.2 1.2 rev.7
  10.3 1.0 add_multiply_fusion
  11.3 0.4 convolution_multiply_fusion
  11.7 10.0 %fusion = f32[32,1024]{1,0:T(8,128)S(1)} fusion(f32[32,2048]{1,0:T(8,128)S(1)} %add_multiply_fusion, f32[1024,2048]{1,0:T(8,128)} %param.3), kind=kOutput, calls=%fused_computation.4 | convolution fusion | flops 805306368 | bytes 8781824 | tf_op jit(solution)/shard_map/dot_general | solution.py:27
  21.7 2.0 %all-gather = f32[64,1024]{1,0:T(8,128)S(1)} all-gather(f32[32,1024]{1,0:T(8,128)S(1)} %fusion), channel_id=2, replica_groups=mesh['grp'=2,'scan'=8,'det'=2] {'det'}, dimensions={0}, use_global_device_ids=true | all-gather | bytes 393216 | tf_op jit(solution)/shard_map/all_gather | solution.py:22
  23.7 0.0 copy-done.1
  23.7 0.3 convolution_divide_fusion
  24.0 0.0 copy-start
  24.0 7.9 %fusion.1 = f32[32,2048]{1,0:T(8,128)} fusion(f32[32,1024]{1,0:T(8,128)S(1)} %convolution_divide_fusion, f32[1024,2048]{1,0:T(8,128)} %param.3), kind=kOutput, calls=%fused_computation.5 | convolution fusion | flops 805306368 | bytes 8781824 | tf_op jit(solution)/shard_map/dot_general | solution.py:31
  31.9 0.0 all-reduce.2.cloned.1.call-update
  31.9 73.7 %all-reduce.2.cloned.1.call-done = f32[32,2048]{1,0:T(8,128)} async-done(((f32[32,2048]{1,0:T(8,128)}), f32[32,2048]{1,0:T(8,128)}) %all-reduce.2.cloned.1.call-update) | async-done | bytes 262160 | tf_op jit(solution)/shard_map/psum | solution.py:35
  105.7 0.0 collective-permute-start.1
  105.7 0.2 fusion.2
  105.9 35.3 %psum.15 = f32[32,32]{1,0:T(8,128)S(1)} all-reduce(f32[32,32]{1,0:T(8,128)S(1)} %fusion.2), channel_id=1, replica_groups=mesh['grp'=2,'scan'=8,'det'=2] {'scan'}, use_global_device_ids=true, to_apply=%region_2.3 | all-reduce | flops 1024 | bytes 8192 | tf_op jit(solution)/shard_map/psum | solution.py:35
  141.2 0.0 collective-permute-done.1
  141.2 1.2 rev.8
  142.4 2.0 %multiply_divide_fusion = f32[32,2048]{1,0:T(8,128)} fusion(f32[32,2048]{1,0:T(8,128)S(1)} %add_multiply_fusion, f32[32,2048]{1,0:T(8,128)} %all-reduce.2.cloned.1.call-done, f32[32,2048]{1,0:T(8,128)S(1)} %rev.8, f32[32,32]{1,0:T(8,128)S(1)} %psum.15), kind=kOutput, calls=%fused_computation.2 | convolution fusion | flops 25427968 | bytes 1052672 | tf_op jit(solution)/shard_map/dot_general | solution.py:38
  144.4 0.0 copy-done
  (1 shorter events, 0.0 us)
Async XLA Ops:
  7.2 16.5 %copy-start.1 = (f32[32,1024]{1,0:T(8,128)S(1)}, f32[32,1024]{1,0:T(8,128)}, u32[]{:S(2)}) copy-start(f32[32,1024]{1,0:T(8,128)} %param.5) | copy-start | bytes 393220
  7.2 98.5 %all-reduce.2.cloned.1.call-start = ((), (), s32[]{:S(2)}) async-start(), calls=%async_computation | async-start | bytes 524288 | tf_op jit(solution)/shard_map/psum | solution.py:35
  7.2 1.9 %collective-permute-start = (f32[32,2048]{1,0:T(8,128)}, f32[32,2048]{1,0:T(8,128)S(1)}, u32[]{:S(2)}, u32[]{:S(2)}) collective-permute-start(f32[32,2048]{1,0:T(8,128)} %param.4), channel_id=1, source_target_pairs={{0,1},{1,0},{2,3},{3,2},{4,5},{5,4},{6,7},{7,6},{8,9},{9,8},{10,11... | collective-permute-start | bytes 786440 | tf_op jit(solution)/shard_map/ppermute | solution.py:16
  24.0 120.5 %copy-start = (f32[32,1024]{1,0:T(8,128)}, f32[32,1024]{1,0:T(8,128)S(1)}, u32[]{:S(2)}) copy-start(f32[32,1024]{1,0:T(8,128)S(1)} %convolution_divide_fusion) | copy-start | bytes 393220
  105.7 35.6 %collective-permute-start.1 = (f32[32,2048]{1,0:T(8,128)}, f32[32,2048]{1,0:T(8,128)S(1)}, u32[]{:S(2)}, u32[]{:S(2)}) collective-permute-start(f32[32,2048]{1,0:T(8,128)} %all-reduce.2.cloned.1.call-done), channel_id=1, source_target_pairs={{0,1},{1,0},{2,3},{3,2},{4,5},{5,4},{6,7},{7,6},{8,9},{9,8},{10,11... | collective-permute-start | bytes 786440 | tf_op jit(solution)/shard_map/ppermute | solution.py:16
Sparse Core Ops, SparseCore 0:
  32.0 73.5 all-reduce.1
